TPU v7x, 32 devices: a whole 2x2x4 slice. The times are simulated.
32 devices in a mesh: sym: 2 (over core), rad: 16 (over z, y, x).
Axes of the slice: x: 2, y: 2, z: 4, core: 2. Of those that a mesh axis runs over, the one named last changes fastest.
Arguments:
- start_amplitudes: float32 [2, 768, 16, 128], P('sym', None, 'rad'), may hold values from -6 to 6
- coupling: bfloat16 [2, 3, 768, 3, 768], P('sym'), may hold values from -0.078125 to 0.078125
- block_pattern: int32 [2, 6, 3, 6], P('sym'), may hold values 0 or 1
- counts: int32 [2], P('sym'), may hold values from 256 to 768, as said below
- radial_terms: float32 [3, 256], P(None, 'rad'), may hold values from 0.5 to 2
- energy: float32 [2, 768], P('sym'), may hold values from -3 to 3
- potential: float32 [256], replicated, may hold values from -3.140625 to 3.140625
- element_matrices: float32 [2, 2, 128, 128], replicated, may hold values from -0.375 to 0.375
Outputs:
- end_amplitudes: float32 [2, 768, 16, 128], P('sym', None, 'rad')
Inputs may be any that keep to these rules, and one draw needn't show every extreme that they name: `counts`: some symmetry has exactly 768 live channels in every draw.
All inputs are finite; a program needn't handle non-finite values. No bound on the sum of `block_pattern` on one device may be relied on, other than what follows from the above.
Results may differ from a plain program's by a relative error of at most 0.0029.
Values may be sent and summed in bfloat16 or wider, within the bound.
No kernel may reach another device: no remote copies, remote signals or barrier semaphores. Data moves between devices by JAX's collectives and lax.ppermute only.
A program may use at most 128 MiB of HBM per device.

v0:
```python
import jax
import jax.numpy as jnp
from jax import lax
from jax.sharding import PartitionSpec as P

TIME_STEPS = 2


step_length = 0.8


def extended(x, sides, width):
    for axis, dim in sides:
        size, length = (lax.axis_size(axis), x.shape[dim])
        up = [(i, (i + 1) % size) for i in range(size - 1)]
        down = [(j, i) for i, j in up]
        last = lax.slice_in_dim(x, length - width, length, axis=dim)
        initial = lax.slice_in_dim(x, 0, width, axis=dim)
        before = lax.ppermute(last, axis, up)
        after = lax.ppermute(initial, axis, down)
        x = jnp.concatenate([before, x, after], axis=dim)
    return x


def element_product(real_part, imag_part, matrices):
    shape_in = real_part.shape
    elements = matrices.shape[1]
    width = matrices.shape[2]
    real_blocks = real_part.reshape(shape_in[:-1] + (elements, width))
    imag_blocks = imag_part.reshape(shape_in[:-1] + (elements, width))
    highest = lax.Precision.HIGHEST
    out_real = jnp.einsum(
        "abnej,eij->abnei", real_blocks, matrices[0], precision=highest
    ) - jnp.einsum("abnej,eij->abnei", imag_blocks, matrices[1], precision=highest)
    out_imag = jnp.einsum(
        "abnej,eij->abnei", imag_blocks, matrices[0], precision=highest
    ) + jnp.einsum("abnej,eij->abnei", real_blocks, matrices[1], precision=highest)
    return (out_real.reshape(shape_in), out_imag.reshape(shape_in))


def radial_half(channel_block, cosine, sine, matrices):
    real_part = channel_block[:, :, :, 0, :]
    imag_part = channel_block[:, :, :, 1, :]
    turned_real = real_part * cosine + imag_part * sine
    turned_imag = imag_part * cosine - real_part * sine
    out_real, out_imag = element_product(turned_real, turned_imag, matrices)
    return jnp.stack((out_real, out_imag), axis=3)


def shards(
    start_amplitudes,
    coupling,
    block_pattern,
    counts,
    radial_terms,
    energy,
    potential,
    element_matrices,
):
    capacity = coupling.shape[2]
    orders = coupling.shape[1]
    tile_size = capacity // block_pattern.shape[1]
    pattern = jnp.repeat(jnp.repeat(block_pattern[0], tile_size, axis=0), tile_size, axis=2).astype(
        jnp.bfloat16
    )
    weights = (coupling[0] * pattern[None]).reshape(orders * capacity, 3 * capacity)
    live_rows = (
        (jnp.arange(capacity, dtype=jnp.int32) < counts[0])
        .astype(jnp.float32)
        .reshape(1, capacity, 1, 1)
    )
    columns = start_amplitudes.shape[3]
    block_points = radial_terms.shape[1]
    states = columns // (2 * block_points)
    points = potential.shape[0]
    blocks_all = points // block_points
    per_device = capacity // lax.axis_size("rad")
    first_row = lax.axis_index("rad") * per_device
    local_energy = lax.dynamic_slice_in_dim(energy[0], first_row, per_device)
    angles = local_energy[:, None] + potential[None, :]
    cosine = jnp.cos(angles)[None, :, None, :]
    sine = jnp.sin(angles)[None, :, None, :]
    radial_rows = jnp.broadcast_to(
        radial_terms[:, None, None, :], (orders, states, 2, block_points)
    ).reshape(orders, 1, columns)
    out_index = jnp.arange(columns, dtype=jnp.int32)
    out_part = out_index // block_points % 2
    in_index = out_index[:, None]
    swap_sign = jnp.where(
        (in_index == out_index[None, :] + block_points) & (out_part[None, :] == 0), 1.0, 0.0
    )
    swap_sign = swap_sign - jnp.where(
        (in_index == out_index[None, :] - block_points) & (out_part[None, :] == 1), 1.0, 0.0
    )
    swap_sign = swap_sign.astype(jnp.float32)

    def coupled_term(current):
        sent = current.astype(jnp.bfloat16)
        widened = extended(sent, (("sym", 0),), 1)
        product = jnp.dot(
            weights, widened.reshape(3 * capacity, columns), preferred_element_type=jnp.float32
        )
        product = product.reshape(orders, capacity, columns)
        coupled = jnp.sum(product * radial_rows, axis=0)
        return coupled.reshape(1, capacity, 1, columns) * live_rows

    def relay_block(amplitudes, repeats):
        channel_block = lax.all_to_all(amplitudes, "rad", split_axis=1, concat_axis=2, tiled=True)
        items = channel_block.shape[0]
        spread = channel_block.reshape(items, per_device, blocks_all, states, 2, block_points)
        spread = spread.transpose(0, 1, 3, 4, 2, 5).reshape(items, per_device, states, 2, points)
        for repeat_index in range(repeats):
            spread = radial_half(spread, cosine, sine, element_matrices)
        folded = spread.reshape(items, per_device, states, 2, blocks_all, block_points)
        moved = folded.transpose(0, 1, 4, 2, 3, 5).reshape(items, per_device, blocks_all, columns)
        return lax.all_to_all(moved, "rad", split_axis=2, concat_axis=1, tiled=True)

    amplitudes = start_amplitudes * live_rows
    amplitudes = relay_block(amplitudes, 1)
    for step_index in range(TIME_STEPS):
        first = step_length * coupled_term(amplitudes)
        second = step_length / 2.0 * coupled_term(first)
        third = step_length / 3.0 * coupled_term(second)
        even_sum = amplitudes - second
        odd_sum = (first - third).reshape(capacity, columns)
        turned = jnp.dot(
            odd_sum, swap_sign, precision=lax.Precision.HIGHEST, preferred_element_type=jnp.float32
        )
        amplitudes = even_sum + turned.reshape(1, capacity, 1, columns)
        amplitudes = relay_block(amplitudes, 1 if step_index + 1 == TIME_STEPS else 2)
    return amplitudes


def solution(mesh):
    return jax.shard_map(
        shards,
        mesh=mesh,
        in_specs=(
            P("sym", None, "rad", None),
            P("sym", None, None, None, None),
            P("sym", None, None, None),
            P("sym"),
            P(None, "rad"),
            P("sym", None),
            P(),
            P(),
        ),
        out_specs=P("sym", None, "rad", None),
        check_vma=False,
    )
```

profile of v0, /device:TPU:0, one launch (start us, length us, event | category | flops | bytes accessed | tf_op | source)
XLA Modules:
  0.0 197.8 jit_solution(230425637695562630)
XLA Ops:
  0.7 1.9 broadcast_multiply_fusion.1
  2.6 8.3 %all-to-all-start = ((f32[1,768,1,128]{3,2,0,1:T(1,128)}), f32[1,768,1,128]{3,2,0,1:T(1,128)S(1)}, u32[]{:S(2)}, u32[]{:S(2)}) async-start(f32[1,768,1,128]{3,2,0,1:T(1,128)} %bitcast.2), calls=%async_computation | async-start | bytes 786432 | tf_op jit(solution)/shard_map/all_to_all | solution.py:108
  12.1 11.5 %all-to-all-done = f32[1,768,1,128]{3,2,0,1:T(1,128)S(1)} async-done(((f32[1,768,1,128]{3,2,0,1:T(1,128)}), f32[1,768,1,128]{3,2,0,1:T(1,128)S(1)}, u32[]{:S(2)}, u32[]{:S(2)}) %all-to-all-start) | async-done | bytes 393248 | tf_op jit(solution)/shard_map/all_to_all | solution.py:108
  24.6 1.3 fusion.56
  25.9 1.3 fusion.60
  28.6 1.1 copy.174
  29.7 3.6 %all-to-all-start.1 = ((f32[1,48,16,128]{3,1,0,2:T(8,128)}), f32[1,48,16,128]{3,1,0,2:T(8,128)S(1)}, u32[]{:S(2)}, u32[]{:S(2)}) async-start(f32[1,48,16,128]{3,1,0,2:T(8,128)} %copy.174), calls=%async_computation.1 | async-start | bytes 786432 | tf_op jit(solution)/shard_map/all_to_all | solution.py:116
  33.3 15.5 %copy.177 = bf16[1,3,768,3,768]{2,4,3,1,0:T(8,128)(2,1)} copy(bf16[1,3,768,3,768]{4,2,3,1,0:T(8,128)(2,1)} %param.9) | data formatting | bytes 21233664 | tf_op args[1]
  49.2 1.3 collective-permute-start.1
  50.5 3.0 %collective-permute-start = (bf16[1,768,1,128]{3,1,2,0:T(8,128)(2,1)S(1)}, bf16[1,768,1,128]{3,1,2,0:T(8,128)(2,1)S(1)}, u32[]{:S(2)}, u32[]{:S(2)}) collective-permute-start(bf16[1,768,1,128]{3,1,2,0:T(8,128)(2,1)S(1)} %bitcast.309), channel_id=1, source_target_pairs={{0,16},{1,17},{2,18},{3,19},{4,20},{5,21},{6,22},{7,23},{8,24},{9,... | collective-permute-start | bytes 589832 | tf_op jit(solution)/shard_map/ppermute | solution.py:19
  53.8 9.8 %broadcast_multiply_fusion = bf16[1,3,768,3,768]{2,4,3,1,0:T(8,128)(2,1)} fusion(bf16[1,3,768,3,768]{2,4,3,1,0:T(8,128)(2,1)} %copy.177, bf16[768,3,768]{0,2,1:T(8,128)(2,1)S(1)} %bitcast.254), kind=kLoop, calls=%fused_computation | loop fusion | flops 5308416 | bytes 24772608 | tf_op jit(solution)/shard_map/mul | solution.py:66
  63.8 7.2 %fusion = f32[768,128]{1,0:T(8,128)S(1)} fusion(bf16[3,768,2304]{1,2,0:T(8,128)(2,1)} %bitcast.255, bf16[2304,128,1]{1,0,2:T(8,128)(2,1)S(1)} %bitcast.321, f32[3,128]{1,0:T(4,128)S(1)} %mul.418), kind=kOutput, calls=%fused_computation.7 | convolution fusion | flops 1359446016 | bytes 11601408 | tf_op jit(solution)/shard_map/dot_general | solution.py:100
  71.2 1.3 collective-permute-start.3
  72.5 3.0 %collective-permute-start.2 = (bf16[1,768,1,128]{3,1,2,0:T(8,128)(2,1)S(1)}, bf16[1,768,1,128]{3,1,2,0:T(8,128)(2,1)S(1)}, u32[]{:S(2)}, u32[]{:S(2)}) collective-permute-start(bf16[1,768,1,128]{3,1,2,0:T(8,128)(2,1)S(1)} %fusion.21), channel_id=1, source_target_pairs={{0,16},{1,17},{2,18},{3,19},{4,20},{5,21},{6,22},{7,23},{8,24},{9,... | collective-permute-start | bytes 589832 | tf_op jit(solution)/shard_map/ppermute | solution.py:19
  76.7 3.0 %fusion.1 = f32[768,128]{1,0:T(8,128)S(1)} fusion(bf16[3,768,2304]{1,2,0:T(8,128)(2,1)S(1)} %bitcast.257, bf16[2304,128,1]{1,0,2:T(8,128)(2,1)S(1)} %bitcast.322, f32[3,128]{1,0:T(4,128)S(1)} %mul.418), kind=kOutput, calls=%fused_computation.8 | convolution fusion | flops 1359446016 | bytes 11601408 | tf_op jit(solution)/shard_map/dot_general | solution.py:100
  79.9 1.3 collective-permute-start.5
  81.2 3.2 %collective-permute-start.4 = (bf16[1,768,1,128]{3,1,2,0:T(8,128)(2,1)S(1)}, bf16[1,768,1,128]{3,1,2,0:T(8,128)(2,1)S(1)}, u32[]{:S(2)}, u32[]{:S(2)}) collective-permute-start(bf16[1,768,1,128]{3,1,2,0:T(8,128)(2,1)S(1)} %fusion.19), channel_id=1, source_target_pairs={{0,16},{1,17},{2,18},{3,19},{4,20},{5,21},{6,22},{7,23},{8,24},{9,... | collective-permute-start | bytes 589832 | tf_op jit(solution)/shard_map/ppermute | solution.py:19
  85.3 3.0 %fusion.2 = f32[768,128]{1,0:T(8,128)S(1)} fusion(bf16[3,768,2304]{1,2,0:T(8,128)(2,1)S(1)} %bitcast.258, bf16[2304,128,1]{1,0,2:T(8,128)(2,1)S(1)} %bitcast.323, f32[3,128]{1,0:T(4,128)S(1)} %mul.418), kind=kOutput, calls=%fused_computation.9 | convolution fusion | flops 1359446016 | bytes 11601408 | tf_op jit(solution)/shard_map/dot_general | solution.py:100
  88.9 19.8 %all_to_all.99 = f32[1,768,1,128]{3,2,0,1:T(1,128)S(1)} all-to-all(f32[1,768,1,128]{3,2,0,1:T(1,128)S(1)} %bitcast.299), channel_id=1, replica_groups=mesh['sym'=2,'rad'=16] {'rad'}, dimensions={1} | all-to-all | bytes 786432 | tf_op jit(solution)/shard_map/all_to_all | solution.py:108
  113.7 1.1 copy.193
  114.8 15.7 %all_to_all.100 = f32[1,48,16,128]{3,1,0,2:T(8,128)S(1)} all-to-all(f32[1,48,16,128]{3,1,0,2:T(8,128)} %copy.193), channel_id=1, replica_groups=mesh['sym'=2,'rad'=16] {'rad'}, dimensions={2} | all-to-all | bytes 786432 | tf_op jit(solution)/shard_map/all_to_all | solution.py:116
  130.5 1.6 collective-permute-start.7
  132.0 3.0 %collective-permute-start.6 = (bf16[1,768,1,128]{3,1,2,0:T(8,128)(2,1)S(1)}, bf16[1,768,1,128]{3,1,2,0:T(8,128)(2,1)S(1)}, u32[]{:S(2)}, u32[]{:S(2)}) collective-permute-start(bf16[1,768,1,128]{3,1,2,0:T(8,128)(2,1)S(1)} %bitcast.312), channel_id=1, source_target_pairs={{0,16},{1,17},{2,18},{3,19},{4,20},{5,21},{6,22},{7,23},{8,24},{9,... | collective-permute-start | bytes 589832 | tf_op jit(solution)/shard_map/ppermute | solution.py:19
  136.2 7.2 %fusion.3 = f32[768,128]{1,0:T(8,128)S(1)} fusion(bf16[3,768,2304]{1,2,0:T(8,128)(2,1)} %bitcast.256, bf16[2304,128,1]{1,0,2:T(8,128)(2,1)S(1)} %bitcast.324, f32[3,128]{1,0:T(4,128)S(1)} %copy-done.15), kind=kOutput, calls=%fused_computation.10 | convolution fusion | flops 1359446016 | bytes 11601408 | tf_op jit(solution)/shard_map/dot_general | solution.py:100
  143.6 1.3 collective-permute-start.9
  144.9 3.3 %collective-permute-start.8 = (bf16[1,768,1,128]{3,1,2,0:T(8,128)(2,1)S(1)}, bf16[1,768,1,128]{3,1,2,0:T(8,128)(2,1)S(1)}, u32[]{:S(2)}, u32[]{:S(2)}) collective-permute-start(bf16[1,768,1,128]{3,1,2,0:T(8,128)(2,1)S(1)} %fusion.17), channel_id=1, source_target_pairs={{0,16},{1,17},{2,18},{3,19},{4,20},{5,21},{6,22},{7,23},{8,24},{9,... | collective-permute-start | bytes 589832 | tf_op jit(solution)/shard_map/ppermute | solution.py:19
  149.1 3.0 %fusion.4 = f32[768,128]{1,0:T(8,128)S(1)} fusion(bf16[3,768,2304]{1,2,0:T(8,128)(2,1)S(1)} %bitcast.261, bf16[2304,128,1]{1,0,2:T(8,128)(2,1)S(1)} %bitcast.325, f32[3,128]{1,0:T(4,128)S(1)} %copy-done.15), kind=kOutput, calls=%fused_computation.11 | convolution fusion | flops 1359446016 | bytes 11601408 | tf_op jit(solution)/shard_map/dot_general | solution.py:100
  152.3 1.3 collective-permute-start.11
  153.6 3.0 %collective-permute-start.10 = (bf16[1,768,1,128]{3,1,2,0:T(8,128)(2,1)S(1)}, bf16[1,768,1,128]{3,1,2,0:T(8,128)(2,1)S(1)}, u32[]{:S(2)}, u32[]{:S(2)}) collective-permute-start(bf16[1,768,1,128]{3,1,2,0:T(8,128)(2,1)S(1)} %fusion.15), channel_id=1, source_target_pairs={{0,16},{1,17},{2,18},{3,19},{4,20},{5,21},{6,22},{7,23},{8,24},{9,... | collective-permute-start | bytes 589832 | tf_op jit(solution)/shard_map/ppermute | solution.py:19
  157.8 3.0 %fusion.5 = f32[768,128]{1,0:T(8,128)S(1)} fusion(bf16[3,768,2304]{1,2,0:T(8,128)(2,1)S(1)} %bitcast.262, bf16[2304,128,1]{1,0,2:T(8,128)(2,1)S(1)} %bitcast.320, f32[3,128]{1,0:T(4,128)S(1)} %copy-done.16), kind=kOutput, calls=%fused_computation.12 | convolution fusion | flops 1359446016 | bytes 11601408 | tf_op jit(solution)/shard_map/dot_general | solution.py:100
  161.4 16.6 %all_to_all.101 = f32[1,768,1,128]{3,2,0,1:T(1,128)S(1)} all-to-all(f32[1,768,1,128]{3,2,0,1:T(1,128)S(1)} %bitcast.298), channel_id=1, replica_groups=mesh['sym'=2,'rad'=16] {'rad'}, dimensions={1} | all-to-all | bytes 786432 | tf_op jit(solution)/shard_map/all_to_all | solution.py:108
  181.6 15.5 %all_to_all.102 = f32[1,48,16,128]{3,1,0,2:T(8,128)S(1)} all-to-all(f32[1,48,16,128]{3,1,0,2:T(8,128)S(1)} %copy.209), channel_id=1, replica_groups=mesh['sym'=2,'rad'=16] {'rad'}, dimensions={2} | all-to-all | bytes 786432 | tf_op jit(solution)/shard_map/all_to_all | solution.py:116
  (130 shorter events, 20.0 us)
Async XLA Ops:
  0.0 11.0 %copy-start = (f32[1,768]{1,0:T(1,128)S(1)}, f32[1,768]{1,0:T(1,128)}, u32[]{:S(2)}) copy-start(f32[1,768]{1,0:T(1,128)} %param.13) | copy-start | bytes 9220
  0.0 27.2 %copy-start.2 = (f32[2,2,128,128]{3,2,1,0:T(8,128)S(1)}, f32[2,2,128,128]{3,2,1,0:T(8,128)}, u32[]{:S(2)}) copy-start(f32[2,2,128,128]{3,2,1,0:T(8,128)} %param.15) | copy-start | bytes 786436
  2.6 21.0 %all-to-all-start = ((f32[1,768,1,128]{3,2,0,1:T(1,128)}), f32[1,768,1,128]{3,2,0,1:T(1,128)S(1)}, u32[]{:S(2)}, u32[]{:S(2)}) async-start(f32[1,768,1,128]{3,2,0,1:T(1,128)} %bitcast.2), calls=%async_computation | async-start | bytes 786432 | tf_op jit(solution)/shard_map/all_to_all | solution.py:108
  12.0 97.7 %copy-start.4 = (f32[48,2,128]{2,1,0:T(2,128)}, f32[48,2,128]{2,1,0:T(2,128)S(1)}, u32[]{:S(2)}) copy-start(f32[48,2,128]{2,1,0:T(2,128)S(1)} %copy.166) | copy-start | bytes 147460
  12.1 97.6 %copy-start.6 = (f32[48,2,128]{2,1,0:T(2,128)}, f32[48,2,128]{2,1,0:T(2,128)S(1)}, u32[]{:S(2)}) copy-start(f32[48,2,128]{2,1,0:T(2,128)S(1)} %copy.164) | copy-start | bytes 147460
  29.7 19.4 %all-to-all-start.1 = ((f32[1,48,16,128]{3,1,0,2:T(8,128)}), f32[1,48,16,128]{3,1,0,2:T(8,128)S(1)}, u32[]{:S(2)}, u32[]{:S(2)}) async-start(f32[1,48,16,128]{3,1,0,2:T(8,128)} %copy.174), calls=%async_computation.1 | async-start | bytes 786432 | tf_op jit(solution)/shard_map/all_to_all | solution.py:116
  33.3 15.5 %copy-start.8 = (s32[1,6,3,6]{3,0,2,1:T(1,128)S(1)}, s32[1,6,3,6]{3,0,2,1:T(1,128)}, u32[]{:S(2)}) copy-start(s32[1,6,3,6]{3,0,2,1:T(1,128)} %param.10) | copy-start | bytes 1300
  49.2 14.5 %collective-permute-start.1 = (bf16[1,768,1,128]{3,1,2,0:T(8,128)(2,1)S(1)}, bf16[1,768,1,128]{3,1,2,0:T(8,128)(2,1)S(1)}, u32[]{:S(2)}, u32[]{:S(2)}) collective-permute-start(bf16[1,768,1,128]{3,1,2,0:T(8,128)(2,1)S(1)} %bitcast.308), channel_id=1, source_target_pairs={{16,0},{17,1},{18,2},{19,3},{20,4},{21,5},{22,6},{23,7},{24,8},{25... | collective-permute-start | bytes 589832 | tf_op jit(solution)/shard_map/ppermute | solution.py:20
  50.5 13.3 %collective-permute-start = (bf16[1,768,1,128]{3,1,2,0:T(8,128)(2,1)S(1)}, bf16[1,768,1,128]{3,1,2,0:T(8,128)(2,1)S(1)}, u32[]{:S(2)}, u32[]{:S(2)}) collective-permute-start(bf16[1,768,1,128]{3,1,2,0:T(8,128)(2,1)S(1)} %bitcast.309), channel_id=1, source_target_pairs={{0,16},{1,17},{2,18},{3,19},{4,20},{5,21},{6,22},{7,23},{8,24},{9,... | collective-permute-start | bytes 589832 | tf_op jit(solution)/shard_map/ppermute | solution.py:19
  53.8 9.8 %copy-start.13 = (f32[3,16]{1,0:T(4,128)S(1)}, f32[3,16]{1,0:T(4,128)}, u32[]{:S(2)}) copy-start(f32[3,16]{1,0:T(4,128)} %param.12) | copy-start | bytes 580
  63.7 21.6 %copy-start.14 = (f32[3,128]{1,0:T(4,128)}, f32[3,128]{1,0:T(4,128)S(1)}, u32[]{:S(2)}) copy-start(f32[3,128]{1,0:T(4,128)S(1)} %mul.418) | copy-start | bytes 4612
  63.7 12.9 %copy-start.3 = (bf16[1,3,768,3,768]{2,4,3,1,0:T(8,128)(2,1)S(1)}, bf16[1,3,768,3,768]{2,4,3,1,0:T(8,128)(2,1)}, u32[]{:S(2)}) copy-start(bf16[1,3,768,3,768]{2,4,3,1,0:T(8,128)(2,1)} %broadcast_multiply_fusion) | copy-start | bytes 31850500
  71.2 4.4 %collective-permute-start.3 = (bf16[1,768,1,128]{3,1,2,0:T(8,128)(2,1)S(1)}, bf16[1,768,1,128]{3,1,2,0:T(8,128)(2,1)S(1)}, u32[]{:S(2)}, u32[]{:S(2)}) collective-permute-start(bf16[1,768,1,128]{3,1,2,0:T(8,128)(2,1)S(1)} %fusion.21), channel_id=1, source_target_pairs={{16,0},{17,1},{18,2},{19,3},{20,4},{21,5},{22,6},{23,7},{24,8},{25... | collective-permute-start | bytes 589832 | tf_op jit(solution)/shard_map/ppermute | solution.py:20
  72.5 4.1 %collective-permute-start.2 = (bf16[1,768,1,128]{3,1,2,0:T(8,128)(2,1)S(1)}, bf16[1,768,1,128]{3,1,2,0:T(8,128)(2,1)S(1)}, u32[]{:S(2)}, u32[]{:S(2)}) collective-permute-start(bf16[1,768,1,128]{3,1,2,0:T(8,128)(2,1)S(1)} %fusion.21), channel_id=1, source_target_pairs={{0,16},{1,17},{2,18},{3,19},{4,20},{5,21},{6,22},{7,23},{8,24},{9,... | collective-permute-start | bytes 589832 | tf_op jit(solution)/shard_map/ppermute | solution.py:19
  75.6 12.8 %copy-start.9 = (pred[128]{0:T(512)(128)(4,1)}, pred[128]{0:T(512)(128)(4,1)S(1)}, u32[]{:S(2)}) copy-start(pred[128]{0:T(512)(128)(4,1)S(1)} %get-tuple-element.21) | copy-start | bytes 388
  75.6 12.8 %copy-start.11 = (pred[128]{0:T(512)(128)(4,1)}, pred[128]{0:T(512)(128)(4,1)S(1)}, u32[]{:S(2)}) copy-start(pred[128]{0:T(512)(128)(4,1)S(1)} %get-tuple-element.22) | copy-start | bytes 388
  79.9 4.7 %collective-permute-start.5 = (bf16[1,768,1,128]{3,1,2,0:T(8,128)(2,1)S(1)}, bf16[1,768,1,128]{3,1,2,0:T(8,128)(2,1)S(1)}, u32[]{:S(2)}, u32[]{:S(2)}) collective-permute-start(bf16[1,768,1,128]{3,1,2,0:T(8,128)(2,1)S(1)} %fusion.19), channel_id=1, source_target_pairs={{16,0},{17,1},{18,2},{19,3},{20,4},{21,5},{22,6},{23,7},{24,8},{25... | collective-permute-start | bytes 589832 | tf_op jit(solution)/shard_map/ppermute | solution.py:20
  81.2 4.1 %collective-permute-start.4 = (bf16[1,768,1,128]{3,1,2,0:T(8,128)(2,1)S(1)}, bf16[1,768,1,128]{3,1,2,0:T(8,128)(2,1)S(1)}, u32[]{:S(2)}, u32[]{:S(2)}) collective-permute-start(bf16[1,768,1,128]{3,1,2,0:T(8,128)(2,1)S(1)} %fusion.19), channel_id=1, source_target_pairs={{0,16},{1,17},{2,18},{3,19},{4,20},{5,21},{6,22},{7,23},{8,24},{9,... | collective-permute-start | bytes 589832 | tf_op jit(solution)/shard_map/ppermute | solution.py:19
  109.2 27.0 %copy-start.15 = (f32[3,128]{1,0:T(4,128)S(1)}, f32[3,128]{1,0:T(4,128)}, u32[]{:S(2)}) copy-start(f32[3,128]{1,0:T(4,128)} %copy-done.14) | copy-start | bytes 4612
  113.4 35.6 %slice-start = ((s8[10616832]{0:T(1024)(128)(4,1)}), s8[2228224]{0:T(1024)(128)(4,1)S(1)}, s32[]{:S(2)}) async-start(s8[10616832]{0:T(1024)(128)(4,1)} %bitcast.259), calls=%async_computation.6 | async-start | bytes 4456448
  130.5 18.6 %slice-start.1 = ((s8[10616832]{0:T(1024)(128)(4,1)}), s8[4194304]{0:T(1024)(128)(4,1)S(1)}, s32[]{:S(2)}) async-start(s8[10616832]{0:T(1024)(128)(4,1)} %bitcast.259), calls=%async_computation.7 | async-start | bytes 8388608
  130.5 4.6 %collective-permute-start.7 = (bf16[1,768,1,128]{3,1,2,0:T(8,128)(2,1)S(1)}, bf16[1,768,1,128]{3,1,2,0:T(8,128)(2,1)S(1)}, u32[]{:S(2)}, u32[]{:S(2)}) collective-permute-start(bf16[1,768,1,128]{3,1,2,0:T(8,128)(2,1)S(1)} %bitcast.311), channel_id=1, source_target_pairs={{16,0},{17,1},{18,2},{19,3},{20,4},{21,5},{22,6},{23,7},{24,8},{25... | collective-permute-start | bytes 589832 | tf_op jit(solution)/shard_map/ppermute | solution.py:20
  132.0 4.1 %collective-permute-start.6 = (bf16[1,768,1,128]{3,1,2,0:T(8,128)(2,1)S(1)}, bf16[1,768,1,128]{3,1,2,0:T(8,128)(2,1)S(1)}, u32[]{:S(2)}, u32[]{:S(2)}) collective-permute-start(bf16[1,768,1,128]{3,1,2,0:T(8,128)(2,1)S(1)} %bitcast.312), channel_id=1, source_target_pairs={{0,16},{1,17},{2,18},{3,19},{4,20},{5,21},{6,22},{7,23},{8,24},{9,... | collective-permute-start | bytes 589832 | tf_op jit(solution)/shard_map/ppermute | solution.py:19
  136.2 12.9 %slice-start.2 = ((s8[10616832]{0:T(1024)(128)(4,1)}), s8[4194304]{0:T(1024)(128)(4,1)S(1)}, s32[]{:S(2)}) async-start(s8[10616832]{0:T(1024)(128)(4,1)} %bitcast.259), calls=%async_computation.8 | async-start | bytes 8388608
  143.4 14.4 %copy-start.16 = (f32[3,128]{1,0:T(4,128)S(1)}, f32[3,128]{1,0:T(4,128)}, u32[]{:S(2)}) copy-start(f32[3,128]{1,0:T(4,128)} %copy-done.14) | copy-start | bytes 4612
  143.6 4.6 %collective-permute-start.9 = (bf16[1,768,1,128]{3,1,2,0:T(8,128)(2,1)S(1)}, bf16[1,768,1,128]{3,1,2,0:T(8,128)(2,1)S(1)}, u32[]{:S(2)}, u32[]{:S(2)}) collective-permute-start(bf16[1,768,1,128]{3,1,2,0:T(8,128)(2,1)S(1)} %fusion.17), channel_id=1, source_target_pairs={{16,0},{17,1},{18,2},{19,3},{20,4},{21,5},{22,6},{23,7},{24,8},{25... | collective-permute-start | bytes 589832 | tf_op jit(solution)/shard_map/ppermute | solution.py:20
  144.9 4.1 %collective-permute-start.8 = (bf16[1,768,1,128]{3,1,2,0:T(8,128)(2,1)S(1)}, bf16[1,768,1,128]{3,1,2,0:T(8,128)(2,1)S(1)}, u32[]{:S(2)}, u32[]{:S(2)}) collective-permute-start(bf16[1,768,1,128]{3,1,2,0:T(8,128)(2,1)S(1)} %fusion.17), channel_id=1, source_target_pairs={{0,16},{1,17},{2,18},{3,19},{4,20},{5,21},{6,22},{7,23},{8,24},{9,... | collective-permute-start | bytes 589832 | tf_op jit(solution)/shard_map/ppermute | solution.py:19
  152.3 4.5 %collective-permute-start.11 = (bf16[1,768,1,128]{3,1,2,0:T(8,128)(2,1)S(1)}, bf16[1,768,1,128]{3,1,2,0:T(8,128)(2,1)S(1)}, u32[]{:S(2)}, u32[]{:S(2)}) collective-permute-start(bf16[1,768,1,128]{3,1,2,0:T(8,128)(2,1)S(1)} %fusion.15), channel_id=1, source_target_pairs={{16,0},{17,1},{18,2},{19,3},{20,4},{21,5},{22,6},{23,7},{24,8},{25... | collective-permute-start | bytes 589832 | tf_op jit(solution)/shard_map/ppermute | solution.py:20
  153.6 4.1 %collective-permute-start.10 = (bf16[1,768,1,128]{3,1,2,0:T(8,128)(2,1)S(1)}, bf16[1,768,1,128]{3,1,2,0:T(8,128)(2,1)S(1)}, u32[]{:S(2)}, u32[]{:S(2)}) collective-permute-start(bf16[1,768,1,128]{3,1,2,0:T(8,128)(2,1)S(1)} %fusion.15), channel_id=1, source_target_pairs={{0,16},{1,17},{2,18},{3,19},{4,20},{5,21},{6,22},{7,23},{8,24},{9,... | collective-permute-start | bytes 589832 | tf_op jit(solution)/shard_map/ppermute | solution.py:19
  157.8 21.1 %copy-start.5 = (f32[48,2,128]{2,1,0:T(2,128)S(1)}, f32[48,2,128]{2,1,0:T(2,128)}, u32[]{:S(2)}) copy-start(f32[48,2,128]{2,1,0:T(2,128)} %copy-done.4) | copy-start | bytes 147460
  157.8 21.1 %copy-start.7 = (f32[48,2,128]{2,1,0:T(2,128)S(1)}, f32[48,2,128]{2,1,0:T(2,128)}, u32[]{:S(2)}) copy-start(f32[48,2,128]{2,1,0:T(2,128)} %copy-done.6) | copy-start | bytes 147460
  157.8 39.9 %copy-start.1 = (f32[1,768]{1,0:T(1,128)S(1)}, f32[1,768]{1,0:T(1,128)}, u32[]{:S(2)}) copy-start(f32[1,768]{1,0:T(1,128)} %param.13) | copy-start | bytes 9220
  (2 other events, 17.5 us)
where the time goes:
time: 199 us; the launch traced here: 198 us
  blocking collectives  67.5 us (34%)
  starting transfers between devices  38.7 us (19%)
  matrix products  35.6 us (18%)
  local copies, waits for them, and re-layouts  23.8 us (12%)
  waiting for transfers between devices  15.9 us (8%)
  other arithmetic  14.6 us (7%)
    all_to_all x2, blocking collectives, relay_block(): lax.all_to_all(amplitudes, 'rad', split_axis=1, concat_axis=2, tiled=True)  36.4 us
    all_to_all x2, blocking collectives, relay_block(): return lax.all_to_all(moved, 'rad', split_axis=2, concat_axis=1, tiled=True)  31.1 us
    dot_general x6, matrix products, coupled_term(): jnp.dot(weights, widened.reshape(3 * capacity, columns), preferred_elemen...  26.5 us
    ppermute x6, starting transfers between devices, extended(): before = lax.ppermute(last, axis, up)  18.7 us
    unnamed x42, local copies, waits for them, and re-layouts  16.4 us
    all_to_all x1, waiting for transfers between devices, relay_block(): lax.all_to_all(amplitudes, 'rad', split_axis=1, concat_axis=2, tiled=True)  11.5 us
    mul x1, other arithmetic, shards(): coupling[0] * pattern[None]  9.82 us
    all_to_all x1, starting transfers between devices, relay_block(): lax.all_to_all(amplitudes, 'rad', split_axis=1, concat_axis=2, tiled=True)  8.34 us
  transfers between devices with their start and end apart: 14, of which 6 were waited for; matrix products, arithmetic and copies ran while one was open for 14% of the time, Pallas kernels for 0%

commit v1 on v0

--- a/solution.py
+++ b/solution.py
@@ -1,6 +1,8 @@
 import jax
 import jax.numpy as jnp
 from jax import lax
+from jax.experimental import pallas as pl
+from jax.experimental.pallas import tpu as pltpu
 from jax.sharding import PartitionSpec as P
 
 TIME_STEPS = 2
@@ -47,7 +49,7 @@
     return jnp.stack((out_real, out_imag), axis=3)
 
 
-def shards(
+def halo_shards(
     start_amplitudes,
     coupling,
     block_pattern,
@@ -131,9 +133,330 @@
     return amplitudes
 
 
+f32 = jnp.float32
+bf16 = jnp.bfloat16
+f16 = jnp.float16
+NT = (((1,), (1,)), ((), ()))
+
+
+def halves(x):
+    high = x.astype(bf16)
+    return high, (x - high.astype(f32)).astype(bf16)
+
+
+def split_dot(a, b):
+    a0, a1 = halves(a)
+    b0, b1 = halves(b)
+
+    def mm(x, y):
+        return lax.dot_general(x, y, NT, preferred_element_type=f32)
+
+    return mm(a0, b0) + (mm(a0, b1) + mm(a1, b0))
+
+
+def pack_kernel(count_ref, start_ref, radial_ref, out_ref):
+    capacity, columns = start_ref.shape
+    states, rows, width = out_ref.shape
+    row = lax.broadcasted_iota(jnp.int32, (capacity, columns), 0)
+    live = jnp.where(row < count_ref[0], start_ref[...], 0.0)
+    out_ref[:, :, :capacity] = live.T.reshape(states, rows, capacity)
+    for state in range(states):
+        out_ref[state, :, capacity:] = radial_ref[...]
+
+
+def unpack_kernel(in_ref, out_ref):
+    states, rows, capacity = in_ref.shape
+    out_ref[...] = in_ref[...].reshape(states * rows, capacity).astype(f32).T
+
+
+def steps_kernel(
+    orders,
+    block,
+    info_ref,
+    own_w,
+    other_w,
+    own_x,
+    other_x,
+    phase_ref,
+    turn_ref,
+    matrix_ref,
+    out_ref,
+    weights,
+    current,
+    total,
+    factors,
+    phases,
+    one_half,
+    two_half,
+    sems,
+):
+    tiles = weights.shape[1]
+    tile = weights.shape[3]
+    capacity = tiles * tile
+    columns = current.shape[2]
+    width = columns // 2
+    me = info_ref[0]
+    part = info_ref[1]
+    per_slot = tiles * 3 * tiles
+
+    def fetch(a, i, b):
+        k = 1 if a == b else (2 - 2 * me if a == 0 else 2 * me)
+        source = own_w if a == 0 else other_w
+        return pltpu.make_async_copy(
+            source.at[:, k, i * tile : (i + 1) * tile, :],
+            weights.at[a, i, :, :, b * capacity : (b + 1) * capacity],
+            sems.at[a, i, b],
+        )
+
+    for a in range(2):
+        for i in range(tiles):
+            for b in range(2):
+                fetch(a, i, b).start()
+
+    m0 = matrix_ref[0]
+    m1 = matrix_ref[1]
+    cosine = turn_ref[0:1]
+    sine = turn_ref[1:2]
+    k0 = m0 * cosine + m1 * sine
+    k1 = m1 * cosine - m0 * sine
+
+    def store_pair(ref, real, imag):
+        ref[:width, :width] = real
+        ref[:width, width:] = -imag
+        ref[width:, :width] = imag
+        ref[width:, width:] = real
+
+    store_pair(one_half, k0, k1)
+    highest = lax.Precision.HIGHEST
+    square = lambda x, y: jnp.dot(x, y, precision=highest, preferred_element_type=f32)
+    store_pair(two_half, square(k0, k0) - square(k1, k1), square(k0, k1) + square(k1, k0))
+
+    phases[...] = phase_ref[...].T
+
+    def rotated(v, a, col):
+        c = phases[:, 4 * a + col : 4 * a + col + 1]
+        s = phases[:, 4 * a + col + 1 : 4 * a + col + 2]
+        real, imag = v[:, :width], v[:, width:]
+        return jnp.concatenate([real * c + imag * s, imag * c - real * s], axis=1)
+
+    def begin(a, v):
+        total[a * capacity : (a + 1) * capacity] = v
+        current[0, a * capacity : (a + 1) * capacity] = v.astype(bf16)
+
+    for a, x_ref in enumerate((own_x, other_x)):
+        x = x_ref[...]
+        blocks = x.shape[0] // (2 * block)
+        pieces = [
+            x[(2 * n + p) * block : (2 * n + p + 1) * block] for p in range(2) for n in range(blocks)
+        ]
+        turned = jnp.concatenate(pieces, axis=0).T
+        begin(a, rotated(split_dot(turned[:capacity], one_half[...]), a, 0))
+        if a == 0:
+            for l in range(orders):
+                rows = turned[capacity + 3 * l : capacity + 3 * l + 3]
+                factors[l : l + 1] = rows[0:1] + (rows[1:2] + rows[2:3] / 2048.0) / 2048.0
+
+    def couple(slot, factor, ready):
+        radial = [factors[l : l + 1] * factor for l in range(orders)]
+        for a in range(2):
+            count = info_ref[2 + a]
+            for i in range(tiles):
+                if not ready:
+                    for b in range(2):
+                        fetch(a, i, b).wait()
+                    for b in range(2):
+                        k = 1 if a == b else (2 - 2 * me if a == 0 else 2 * me)
+                        for j in range(tiles):
+                            present = info_ref[4 + a * per_slot + (i * 3 + k) * tiles + j]
+                            first = b * capacity + j * tile
+
+                            @pl.when(present == 0)
+                            def _():
+                                weights[a, i, :, :, first : first + tile] = jnp.zeros(
+                                    (orders, tile, tile), bf16
+                                )
+
+                w = weights[a, i].reshape(orders * tile, 2 * capacity)
+                product = jnp.dot(w, current[slot], preferred_element_type=f32)
+                u = product[:tile] * radial[0]
+                for l in range(1, orders):
+                    u = u + product[l * tile : (l + 1) * tile] * radial[l]
+                row = lax.broadcasted_iota(jnp.int32, u.shape, 0) + i * tile
+                u = jnp.where(row < count, u, 0.0)
+                term = jnp.concatenate([u[:, width:], -u[:, :width]], axis=1)
+                first = a * capacity + i * tile
+                total[first : first + tile] += term
+                current[1 - slot, first : first + tile] = term.astype(bf16)
+
+    step_length_over = lambda k: jnp.where(
+        k == 0, step_length, jnp.where(k == 1, step_length / 2.0, step_length / 3.0)
+    )
+    couple(0, step_length, False)
+
+    def later(index, carry):
+        k = lax.rem(index, 3)
+        slot = lax.rem(index, 2)
+
+        @pl.when(k == 0)
+        def _():
+            for a in range(2):
+                v = total[a * capacity : (a + 1) * capacity]
+                v = rotated(split_dot(v, two_half[...]), a, 2)
+                total[a * capacity : (a + 1) * capacity] = v
+                current[slot, a * capacity : (a + 1) * capacity] = v.astype(bf16)
+
+        couple(slot, step_length_over(k), True)
+        return carry
+
+    lax.fori_loop(1, 3 * TIME_STEPS, later, 0)
+
+    final = rotated(total[:capacity], 0, 0)
+    pieces = out_ref.shape[0]
+    spread = width // (block * pieces)
+    for m in range(pieces):
+        for p in range(2):
+            first = pl.multiple_of(p * width + (m * spread + part) * block, block)
+            two_half[(2 * m + p) * block : (2 * m + p + 1) * block] = one_half[pl.ds(first, block)]
+    result = split_dot(two_half[: 2 * pieces * block], final)
+    out_ref[...] = result.astype(bf16).reshape(out_ref.shape)
+
+
+def pair_shards(
+    start_amplitudes,
+    coupling,
+    block_pattern,
+    counts,
+    radial_terms,
+    energy,
+    potential,
+    element_matrices,
+):
+    orders, capacity = coupling.shape[1:3]
+    tiles = block_pattern.shape[1]
+    tile = capacity // tiles
+    columns = start_amplitudes.shape[3]
+    block = radial_terms.shape[1]
+    width = element_matrices.shape[2]
+    elements = element_matrices.shape[1]
+    states = columns // (2 * block)
+    group = width // block
+    spread = group // states
+    rows = 2 * block
+    vmem = pl.BlockSpec(memory_space=pltpu.VMEM)
+    smem = pl.BlockSpec(memory_space=pltpu.SMEM)
+    anywhere = pl.BlockSpec(memory_space=pl.ANY)
+    swap = [(0, 1), (1, 0)]
+    place = lax.axis_index("rad")
+    me = lax.axis_index("sym")
+    element = place // group
+
+    other_coupling = lax.ppermute(coupling, "sym", swap)
+    angle = energy[0]
+    phase = jnp.stack([jnp.cos(angle), jnp.sin(angle), jnp.cos(2.0 * angle), jnp.sin(2.0 * angle)])
+    integers = jnp.concatenate([counts, block_pattern.reshape(-1)]).astype(f32)
+    padded = -(-integers.shape[0] // capacity) * capacity
+    small = jnp.concatenate(
+        [phase, jnp.pad(integers, (0, padded - integers.shape[0])).reshape(-1, capacity)]
+    )
+    other_small = lax.ppermute(small, "sym", swap)
+    other_integers = other_small[4:].reshape(-1)[: integers.shape[0]].astype(jnp.int32)
+    info = jnp.concatenate(
+        [
+            jnp.stack([me, place % spread, counts[0], other_integers[0]]).astype(jnp.int32),
+            block_pattern.reshape(-1),
+            other_integers[1:],
+        ]
+    )
+    lanes = 128
+    phases = jnp.concatenate(
+        [phase, other_small[:4], jnp.zeros((lanes - 8, capacity), f32)]
+    )
+    radii = lax.dynamic_slice_in_dim(potential, element * width, width)
+    turn = jnp.stack([jnp.cos(radii), jnp.sin(radii)])
+    matrices = lax.dynamic_index_in_dim(element_matrices, element, 1, keepdims=False)
+
+    high = lax.reduce_precision(radial_terms, 8, 10)
+    rest = (radial_terms - high) * 2048.0
+    middle = lax.reduce_precision(rest, 8, 10)
+    low = (rest - middle) * 2048.0
+    pieces = jnp.stack([high, middle, low], axis=1).reshape(3 * orders, block).T
+    radial = jnp.pad(jnp.tile(pieces, (2, 1)), ((0, 0), (0, lanes - 3 * orders)))
+
+    packed = pl.pallas_call(
+        pack_kernel,
+        out_shape=jax.ShapeDtypeStruct((states, rows, capacity + lanes), f32),
+        in_specs=[smem, vmem, vmem],
+        out_specs=vmem,
+        name="pack",
+    )(counts, start_amplitudes.reshape(capacity, columns), radial)
+    wide = [[e * group + d for d in range(group)] for e in range(elements)]
+    gathered = lax.all_to_all(
+        jnp.repeat(packed.astype(f16), spread, axis=0), "rad", split_axis=0, concat_axis=0, tiled=True, axis_index_groups=wide
+    ).reshape(group * rows, capacity + lanes)
+    other_gathered = lax.ppermute(gathered, "sym", swap)
+
+    def by_order(x):
+        return x[0].transpose(0, 2, 1, 3)
+
+    scratch = [
+        pltpu.VMEM((2, tiles, orders, tile, 2 * capacity), bf16),
+        pltpu.VMEM((2, 2 * capacity, 2 * width), bf16),
+        pltpu.VMEM((2 * capacity, 2 * width), f32),
+        pltpu.VMEM((8, 2 * width), f32),
+        pltpu.VMEM((capacity, lanes), f32),
+        pltpu.VMEM((2 * width, 2 * width), f32),
+        pltpu.VMEM((2 * width, 2 * width), f32),
+        pltpu.SemaphoreType.DMA((2, tiles, 2)),
+    ]
+
+    def body(*refs):
+        steps_kernel(orders, block, *refs)
+
+    result = pl.pallas_call(
+        body,
+        out_shape=jax.ShapeDtypeStruct((states, rows, capacity), bf16),
+        in_specs=[smem, anywhere, anywhere, vmem, vmem, vmem, vmem, vmem],
+        out_specs=vmem,
+        scratch_shapes=scratch,
+        compiler_params=pltpu.CompilerParams(vmem_limit_bytes=48 << 20),
+        name="steps",
+    )(
+        info,
+        by_order(coupling),
+        by_order(other_coupling),
+        gathered.astype(f32),
+        other_gathered.astype(f32),
+        phases,
+        turn,
+        matrices,
+    )
+    narrow = [
+        [e * group + n * spread + d for n in range(states)]
+        for e in range(elements)
+        for d in range(spread)
+    ]
+    returned = lax.all_to_all(
+        result, "rad", split_axis=0, concat_axis=0, tiled=True, axis_index_groups=narrow
+    )
+    out = pl.pallas_call(
+        unpack_kernel,
+        out_shape=jax.ShapeDtypeStruct((capacity, columns), f32),
+        in_specs=[vmem],
+        out_specs=vmem,
+        name="unpack",
+    )(returned)
+    return out.reshape(start_amplitudes.shape)
+
+
 def solution(mesh):
+    def program(*args):
+        states = args[0].shape[3] // (2 * args[4].shape[1])
+        group = args[7].shape[2] // args[4].shape[1]
+        paired = mesh.shape["sym"] == 2 and group % states == 0
+        return pair_shards(*args) if paired else halo_shards(*args)
+
     return jax.shard_map(
-        shards,
+        program,
         mesh=mesh,
         in_specs=(
             P("sym", None, "rad", None),

time: 199 us -> 81.3 us (0.41)
  blocking collectives: 67.5 us -> 8.82 us
  Pallas kernels: 0 us -> 50.8 us
  matrix products: 35.6 us -> 0 us
  starting transfers between devices: 38.7 us -> 6.51 us
  local copies, waits for them, and re-layouts: 23.8 us -> 2.85 us
  other arithmetic: 14.6 us -> 3.61 us
  waiting for transfers between devices: 15.9 us -> 7.46 us
    all_to_all x4 -> x1, blocking collectives: 67.5 us -> 8.82 us  [pair_shards(): lax.all_to_all(result, 'rad', split_axis=0, concat_axis=0, tiled=True, ax...]
    pallas_call x0 -> x3, Pallas kernels: none -> 50.8 us  [the longest x1 47.1 us: pair_shards(): pl.pallas_call(body, out_shape=jax.ShapeDtypeStruct((states, rows, capaci...]
    dot_general x24 -> x0, matrix products: 35.6 us -> none  [the longest x6 26.5 us: coupled_term(): jnp.dot(weights, widened.reshape(3 * capacity, columns), preferred_elemen...]
    ppermute x12 -> x3, starting transfers between devices: 26.7 us -> 0.74 us  [the longest x1 0.49 us: pair_shards(): other_coupling = lax.ppermute(coupling, 'sym', swap)]
    unnamed x42 -> x2, local copies, waits for them, and re-layouts: 16.4 us -> 0.01 us
    mul x2 -> x0, other arithmetic: 11.7 us -> none  [the longest x1 9.82 us: shards(): coupling[0] * pattern[None]]
    all_to_all x2 -> x1, waiting for transfers between devices: 11.5 us -> 4.24 us  [pair_shards(): lax.all_to_all(jnp.repeat(packed.astype(f16), spread, axis=0), 'rad', spl...]
    all_to_all x2 -> x1, starting transfers between devices: 12 us -> 5.76 us  [pair_shards(): lax.all_to_all(jnp.repeat(packed.astype(f16), spread, axis=0), 'rad', spl...]
  transfers between devices with their start and end apart: 14 -> 4, of which waited for: 6 -> 3; matrix products, arithmetic and copies ran while one was open for 14% -> 8% of each run, Pallas kernels for 0% -> 2%
where the time goes in v1:
time: 81.3 us; the launch traced here: 80.9 us
  Pallas kernels  50.8 us (62%)
  blocking collectives  8.82 us (11%)
  waiting for transfers between devices  7.46 us (9%)
  starting transfers between devices  6.51 us (8%)
  other arithmetic  3.61 us (4%)
  local copies, waits for them, and re-layouts  2.85 us (4%)
    pallas_call x1, Pallas kernels, pair_shards(): pl.pallas_call(body, out_shape=jax.ShapeDtypeStruct((states, rows, capaci...  47.1 us
    all_to_all x1, blocking collectives, pair_shards(): lax.all_to_all(result, 'rad', split_axis=0, concat_axis=0, tiled=True, ax...  8.82 us
    all_to_all x1, starting transfers between devices, pair_shards(): lax.all_to_all(jnp.repeat(packed.astype(f16), spread, axis=0), 'rad', spl...  5.76 us
    all_to_all x1, waiting for transfers between devices, pair_shards(): lax.all_to_all(jnp.repeat(packed.astype(f16), spread, axis=0), 'rad', spl...  4.24 us
    pallas_call x1, Pallas kernels, pair_shards(): pl.pallas_call(pack_kernel, out_shape=jax.ShapeDtypeStruct((states, rows,...  1.94 us
    pallas_call x1, Pallas kernels, pair_shards(): pl.pallas_call(unpack_kernel, out_shape=jax.ShapeDtypeStruct((capacity, c...  1.81 us
    ppermute x1, waiting for transfers between devices, pair_shards(): other_small = lax.ppermute(small, 'sym', swap)  1.7 us
  transfers between devices with their start and end apart: 4, of which 3 were waited for; matrix products, arithmetic and copies ran while one was open for 8% of the time, Pallas kernels for 2%

profile of v1, /device:TPU:0, one launch (start us, length us, event | category | flops | bytes accessed | tf_op | source)
XLA Modules:
  0.0 80.9 jit_solution(17560899229181508411)
XLA Ops:
  0.0 0.0 copy-start
  0.0 0.5 collective-permute-start.1
  1.1 0.7 reduce-precision_bitcast_fusion.1
  1.9 0.1 copy.11
  2.0 0.6 pad.9.radial_ref
  2.6 1.9 %pack.1 = f32[4,32,896]{2,1,0:T(8,128)} custom-call(s32[1]{0:T(128)S(6)} %copy.13.count_ref, f32[768,128]{1,0:T(8,128)} %bitcast.35, f32[32,128]{1,0:T(8,128)} %pad.9.radial_ref), custom_call_target="tpu_custom_call" | custom-call | tf_op jit(solution)/shard_map/pack/pallas_call | solution.py:385
  4.5 1.0 %convert_element_type.22 = f16[4,32,896]{2,1,0:T(8,128)(2,1)S(1)} convert(f32[4,32,896]{2,1,0:T(8,128)} %pack.1) | non-fusion elementwise | flops 114688 | bytes 688128 | tf_op jit(solution)/shard_map/convert_element_type | solution.py:394
  5.6 0.8 %broadcast_in_dim.6 = f16[4,2,32,896]{3,2,1,0:T(8,128)(2,1)} broadcast(f16[4,32,896]{2,1,0:T(8,128)(2,1)S(1)} %convert_element_type.22), dimensions={0,2,3} | broadcast | bytes 688128 | tf_op jit(solution)/shard_map/broadcast_in_dim | solution.py:394
  6.4 5.8 %all-to-all-start = ((f16[8,32,896]{2,1,0:T(8,128)(2,1)}), f16[8,32,896]{2,1,0:T(8,128)(2,1)S(1)}, u32[]{:S(2)}, u32[]{:S(2)}) async-start(f16[8,32,896]{2,1,0:T(8,128)(2,1)} %bitcast.14), calls=%async_computation | async-start | bytes 917504 | tf_op jit(solution)/shard_map/all_to_all | solution.py:393
  12.2 0.7 reduce
  12.9 0.1 reshape.31
  13.0 0.1 add_convert_fusion
  13.1 0.9 %multiply_sine_fusion = (f32[1,768]{1,0:T(1,128)S(1)}, f32[1,768]{1,0:T(1,128)S(1)}, f32[1,768]{1,0:T(1,128)S(1)}, f32[1,768]{1,0:T(1,128)S(1)}) fusion(f32[1,768]{1,0:T(1,128)} %param.13), kind=kLoop, calls=%fused_computation.9 | loop fusion | flops 768 | bytes 15360 | tf_op jit(solution)/shard_map/sin | solution.py:355
  14.0 0.2 collective-permute-start
  14.3 0.8 cosine_bitcast_fusion
  15.0 0.0 copy-done
  15.1 1.7 %collective-permute-done = f32[5,768]{1,0:T(8,128)S(1)} collective-permute-done((f32[5,768]{1,0:T(8,128)S(1)}, f32[5,768]{1,0:T(8,128)S(1)}, u32[]{:S(2)}, u32[]{:S(2)}) %collective-permute-start) | collective-permute-done | bytes 15392 | tf_op jit(solution)/shard_map/ppermute | solution.py:361
  16.8 0.1 concatenate.17.refs_5_
  17.0 4.2 %all-to-all-done = f16[8,32,896]{2,1,0:T(8,128)(2,1)S(1)} async-done(((f16[8,32,896]{2,1,0:T(8,128)(2,1)}), f16[8,32,896]{2,1,0:T(8,128)(2,1)S(1)}, u32[]{:S(2)}, u32[]{:S(2)}) %all-to-all-start) | async-done | bytes 458784 | tf_op jit(solution)/shard_map/all_to_all | solution.py:393
  21.2 0.0 collective-permute-start.2
  21.2 0.1 slice_bitcast_fusion
  21.3 0.1 concatenate.16.refs_0_
  21.4 0.1 bitcast_convert_fusion.refs_3_
  21.5 1.5 %collective-permute-done.2 = f16[256,896]{1,0:T(8,128)(2,1)S(1)} collective-permute-done((f16[256,896]{1,0:T(8,128)(2,1)S(1)}, f16[256,896]{1,0:T(8,128)(2,1)S(1)}, u32[]{:S(2)}, u32[]{:S(2)}) %collective-permute-start.2) | collective-permute-done | bytes 458784 | tf_op jit(solution)/shard_map/ppermute | solution.py:396
  23.1 0.1 convert_element_type.24.refs_4_
  23.1 0.0 collective-permute-done.1
  23.1 47.1 %steps.1 = bf16[4,32,768]{2,1,0:T(8,128)(2,1)S(1)} custom-call(s32[220]{0:T(256)S(1)} %concatenate.16.refs_0_, bf16[3,3,768,768]{3,2,1,0:T(8,128)(2,1)} %bitcast.33, bf16[3,3,768,768]{3,2,1,0:T(8,128)(2,1)} %bitcast.7.refs_2_, f32[256,896]{1,0:T(8,128)S(1)} %bitcast_convert_fusion.refs_3_, f32[256,896]{1,0:T(8,128)S(1)} %convert_element_type.24.refs_4_, ...), custom_call_target="tpu_custom_call" | custom-call | tf_op jit(solution)/shard_map/steps/pallas_call | solution.py:415
  70.2 8.8 %all_to_all.10.in_ref = bf16[4,32,768]{2,1,0:T(8,128)(2,1)} all-to-all(bf16[4,32,768]{2,1,0:T(8,128)(2,1)S(1)} %steps.1), channel_id=1, replica_groups={{0,2,4,6},{1,3,5,7},{8,10,12,14},{9,11,13,15},{16,18,20,22},{17,19,21,2..., dimensions={0} | all-to-all | bytes 393216 | tf_op jit(solution)/shard_map/all_to_all | solution.py:438
  79.1 1.8 %unpack.1 = f32[768,128]{1,0:T(8,128)} custom-call(bf16[4,32,768]{2,1,0:T(8,128)(2,1)} %all_to_all.10.in_ref), custom_call_target="tpu_custom_call" | custom-call | tf_op jit(solution)/shard_map/unpack/pallas_call | solution.py:441
  (12 shorter events, 0.1 us)
Async XLA Ops:
  0.0 15.0 %copy-start = (f32[2,2,128,128]{3,2,1,0:T(8,128)S(1)}, f32[2,2,128,128]{3,2,1,0:T(8,128)}, u32[]{:S(2)}) copy-start(f32[2,2,128,128]{3,2,1,0:T(8,128)} %param.15) | copy-start | bytes 786436
  0.0 23.1 %collective-permute-start.1 = (bf16[1,3,768,3,768]{4,2,3,1,0:T(8,128)(2,1)}, bf16[1,3,768,3,768]{4,2,3,1,0:T(8,128)(2,1)}, u32[]{:S(2)}, u32[]{:S(2)}) collective-permute-start(bf16[1,3,768,3,768]{4,2,3,1,0:T(8,128)(2,1)} %param.9), channel_id=1, source_target_pairs={{0,16},{16,0},{1,17},{17,1},{2,18},{18,2},{3,19},{19,3},{4,20},{20... | collective-permute-start | bytes 31850504 | tf_op jit(solution)/shard_map/ppermute | solution.py:353
  6.4 14.8 %all-to-all-start = ((f16[8,32,896]{2,1,0:T(8,128)(2,1)}), f16[8,32,896]{2,1,0:T(8,128)(2,1)S(1)}, u32[]{:S(2)}, u32[]{:S(2)}) async-start(f16[8,32,896]{2,1,0:T(8,128)(2,1)} %bitcast.14), calls=%async_computation | async-start | bytes 917504 | tf_op jit(solution)/shard_map/all_to_all | solution.py:393
  14.0 2.8 %collective-permute-start = (f32[5,768]{1,0:T(8,128)S(1)}, f32[5,768]{1,0:T(8,128)S(1)}, u32[]{:S(2)}, u32[]{:S(2)}) collective-permute-start(f32[5,768]{1,0:T(8,128)S(1)} %concatenate.15), channel_id=1, source_target_pairs={{0,16},{16,0},{1,17},{17,1},{2,18},{18,2},{3,19},{19,3},{4,20},{20... | collective-permute-start | bytes 46088 | tf_op jit(solution)/shard_map/ppermute | solution.py:361
  21.2 1.8 %collective-permute-start.2 = (f16[256,896]{1,0:T(8,128)(2,1)S(1)}, f16[256,896]{1,0:T(8,128)(2,1)S(1)}, u32[]{:S(2)}, u32[]{:S(2)}) collective-permute-start(f16[256,896]{1,0:T(8,128)(2,1)S(1)} %bitcast.34), channel_id=1, source_target_pairs={{0,16},{16,0},{1,17},{17,1},{2,18},{18,2},{3,19},{19,3},{4,20},{20... | collective-permute-start | bytes 1376264 | tf_op jit(solution)/shard_map/ppermute | solution.py:396
